TPU v7x, 32 devices: a whole 2x2x4 slice. The times are simulated.
32 devices in a mesh: gx: 4 (over z), gy: 4 (over y, x), gz: 2 (over core).
Axes of the slice: x: 2, y: 2, z: 4, core: 2. Of those that a mesh axis runs over, the one named last changes fastest.
Arguments:
- adjoint_residual: float32 [32, 64, 256], P('gx', 'gy', 'gz'), may hold values from -6 to 6
- face_x: float32 [32, 64, 256], P('gx', 'gy', 'gz'), may hold values from 0.03 to 30
- face_y: float32 [32, 64, 256], P('gx', 'gy', 'gz'), may hold values from 0.03 to 30
- face_z: float32 [32, 64, 256], P('gx', 'gy', 'gz'), may hold values from 0.03 to 30
Outputs:
- correction: float32 [32, 64, 256], P('gx', 'gy', 'gz')
All inputs are finite; a program needn't handle non-finite values.
Results may differ from a plain program's by a relative error of at most 0.0001.
Values sent between devices are 32-bit elements; how exact they have to be, the bound alone decides.
No kernel may reach another device: no remote copies, remote signals or barrier semaphores. Data moves between devices by JAX's collectives and lax.ppermute only.
A program may use at most 64 MiB of HBM per device.

v0:
```python
import jax
import jax.numpy as jnp
from jax import lax
from jax.sharding import PartitionSpec as P

LEVELS = 4
COARSE_ITERS = 6
damping = 2.0 / 3.0


def extended(block, sides, width):
    for axis, dim in sides:
        count = lax.axis_size(axis)
        forward = [(i, i + 1) for i in range(count - 1)]
        backward = [(target, source) for source, target in forward]
        low = lax.ppermute(
            lax.slice_in_dim(block, block.shape[dim] - width, None, axis=dim), axis, forward
        )
        high = lax.ppermute(lax.slice_in_dim(block, 0, width, axis=dim), axis, backward)
        block = jnp.concatenate([low, block, high], axis=dim)
    return block


def from_behind(block, axis, distance):
    devices = range(lax.axis_size(axis))
    route = [(i - distance, i) for i in devices if i - distance in devices]
    return lax.ppermute(block, axis, route)


def stencil(padded, field, coefs):
    low_x, high_x, low_y, high_y, low_z, high_z = coefs
    diagonal = low_x + high_x + low_y + high_y + low_z + high_z
    result = diagonal * field - low_x * padded[:-2, 1:-1, 1:-1] - high_x * padded[2:, 1:-1, 1:-1]
    result = result - low_y * padded[1:-1, :-2, 1:-1] - high_y * padded[1:-1, 2:, 1:-1]
    return result - low_z * padded[1:-1, 1:-1, :-2] - high_z * padded[1:-1, 1:-1, 2:]


def operate(field, coefs):
    padded = extended(field, (("gx", 0), ("gy", 1), ("gz", 2)), 1)
    return stencil(padded, field, coefs)


def operate_whole(field, coefs):
    return stencil(jnp.pad(field, 1), field, coefs)


def blocked(values):
    return values.reshape(values.shape[0] // 2, 2, values.shape[1] // 2, 2, values.shape[2] // 2, 2)


def coarse_face(values, dim, parity):
    others = tuple((2 * k + 1 for k in range(3) if k != dim))
    summed = jnp.sum(blocked(values), axis=others)
    return 0.5 * lax.index_in_dim(summed, parity, dim + 1, keepdims=False)


def coarsen(coefs):
    result = []
    for dim in range(3):
        result.append(coarse_face(coefs[2 * dim], dim, 0))
        result.append(coarse_face(coefs[2 * dim + 1], dim, 1))
    return tuple(result)


def restrict(values):
    return jnp.sum(blocked(values), axis=(1, 3, 5))


def prolong(values):
    shape_out = (values.shape[0] * 2, values.shape[1] * 2, values.shape[2] * 2)
    wide = jnp.broadcast_to(
        values[:, None, :, None, :, None],
        (values.shape[0], 2, values.shape[1], 2, values.shape[2], 2),
    )
    return wide.reshape(shape_out)


def total_local(value):
    return value


def conj_grad(rhs, coefs, apply_op, total):
    solution = jnp.zeros_like(rhs)
    remain = rhs
    search = rhs
    norm_now = total(jnp.sum(remain * remain))
    for step in range(COARSE_ITERS):
        image = apply_op(search, coefs)
        alpha = norm_now / total(jnp.sum(search * image))
        solution = solution + alpha * search
        remain = remain - alpha * image
        norm_next = total(jnp.sum(remain * remain))
        search = remain + norm_next / norm_now * search
        norm_now = norm_next
    return solution


def coarse_solve(rhs, coefs):
    part_x, part_y, part_z = rhs.shape
    count_x = lax.axis_size("gx")
    count_y = lax.axis_size("gy")
    count_z = lax.axis_size("gz")
    stacked = jnp.stack((rhs,) + coefs)[None]
    whole = lax.all_gather(stacked, ("gx", "gy", "gz"), axis=0, tiled=True)
    whole = whole.reshape(count_x, count_y, count_z, 7, part_x, part_y, part_z)
    whole = whole.transpose(3, 0, 4, 1, 5, 2, 6).reshape(
        7, count_x * part_x, count_y * part_y, count_z * part_z
    )
    whole_coefs = tuple((whole[k] for k in range(1, 7)))
    solution = conj_grad(whole[0], whole_coefs, operate_whole, total_local)
    starts = (
        lax.axis_index("gx") * part_x,
        lax.axis_index("gy") * part_y,
        lax.axis_index("gz") * part_z,
    )
    return lax.dynamic_slice(solution, starts, (part_x, part_y, part_z))


def cycle(rhs, levels_left, coefs):
    if levels_left == 1:
        return coarse_solve(rhs, coefs)
    diagonal = coefs[0] + coefs[1] + coefs[2] + coefs[3] + coefs[4] + coefs[5]
    field = damping * rhs / diagonal
    field = field + damping * (rhs - operate(field, coefs)) / diagonal
    remain = rhs - operate(field, coefs)
    field = field + prolong(cycle(restrict(remain), levels_left - 1, coarsen(coefs)))
    field = field + damping * (rhs - operate(field, coefs)) / diagonal
    return field


def per_device(adjoint_residual, face_x, face_y, face_z):
    rim_x = from_behind(face_x[:1], "gx", -1)
    rim_y = from_behind(face_y[:, :1], "gy", -1)
    rim_z = from_behind(face_z[:, :, :1], "gz", -1)
    high_x = jnp.concatenate([face_x[1:], rim_x], 0)
    high_y = jnp.concatenate([face_y[:, 1:], rim_y], 1)
    high_z = jnp.concatenate([face_z[:, :, 1:], rim_z], 2)
    coefs = (face_x, high_x, face_y, high_y, face_z, high_z)
    return cycle(adjoint_residual, LEVELS, coefs)


def solution(mesh):
    return jax.shard_map(
        per_device,
        mesh=mesh,
        in_specs=(
            P("gx", "gy", "gz"),
            P("gx", "gy", "gz"),
            P("gx", "gy", "gz"),
            P("gx", "gy", "gz"),
        ),
        out_specs=P("gx", "gy", "gz"),
        check_vma=False,
    )
```

profile of v0, /device:TPU:0, one launch (start us, length us, event | category | flops | bytes accessed | tf_op | source)
XLA Modules:
  0.0 335.5 jit_solution(15201036902934139529)
XLA Ops:
  5.4 6.3 %reshape.224 = f32[4,2,8,2,64,2]{5,4,3,2,1,0:T(8,128)} reshape(f32[8,16,128]{2,1,0:T(8,128)} %param.7) | data formatting | bytes 131072 | tf_op jit(solution)/shard_map/reshape | solution.py:48
  11.7 5.5 %reshape.222 = f32[4,2,8,2,64,2]{5,4,3,2,1,0:T(8,128)} reshape(f32[8,16,128]{2,1,0:T(8,128)S(1)} %copy-done) | data formatting | bytes 131072 | tf_op jit(solution)/shard_map/reshape | solution.py:48
  17.2 2.8 reduce_sum.349
  20.3 2.8 reduce_sum.347
  23.3 5.5 %reshape.220 = f32[4,2,8,2,64,2]{5,4,3,2,1,0:T(8,128)} reshape(f32[8,16,128]{2,1,0:T(8,128)S(1)} %copy-done.2) | data formatting | bytes 131072 | tf_op jit(solution)/shard_map/reshape | solution.py:48
  28.8 2.8 reduce_sum.345
  31.8 5.6 %collective-permute-start.3 = (f32[1,16,128]{2,1,0:T(8,128)S(1)}, f32[1,16,128]{2,1,0:T(8,128)S(1)}, u32[]{:S(2)}, u32[]{:S(2)}) collective-permute-start(f32[1,16,128]{2,1,0:T(8,128)S(1)} %get-tuple-element.49), channel_id=1, source_target_pairs={{0,8},{8,16},{16,24},{1,9},{9,17},{17,25},{2,10},{10,18},{18,26},{... | collective-permute-start | bytes 24584 | tf_op jit(solution)/shard_map/ppermute | solution.py:16
  39.4 3.5 %collective-permute-done.4 = f32[1,16,128]{2,1,0:T(8,128)S(1)} collective-permute-done((f32[1,16,128]{2,1,0:T(8,128)S(1)}, f32[1,16,128]{2,1,0:T(8,128)S(1)}, u32[]{:S(2)}, u32[]{:S(2)}) %collective-permute-start.4) | collective-permute-done | bytes 8224 | tf_op jit(solution)/shard_map/ppermute | solution.py:19
  43.0 4.5 %collective-permute-start.5 = (f32[10,1,128]{2,1,0:T(1,128)S(1)}, f32[10,1,128]{2,1,0:T(1,128)S(1)}, u32[]{:S(2)}, u32[]{:S(2)}) collective-permute-start(f32[10,1,128]{2,1,0:T(1,128)S(1)} %get-tuple-element.42), channel_id=1, source_target_pairs={{0,2},{2,4},{4,6},{1,3},{3,5},{5,7},{8,10},{10,12},{12,14},{9,11},... | collective-permute-start | bytes 15368 | tf_op jit(solution)/shard_map/ppermute | solution.py:16
  49.5 4.3 %collective-permute-done.6 = f32[10,1,128]{2,1,0:T(1,128)S(1)} collective-permute-done((f32[10,1,128]{2,1,0:T(1,128)S(1)}, f32[10,1,128]{2,1,0:T(1,128)S(1)}, u32[]{:S(2)}, u32[]{:S(2)}) %collective-permute-start.6) | collective-permute-done | bytes 5152 | tf_op jit(solution)/shard_map/ppermute | solution.py:19
  60.0 4.5 %collective-permute-start.9 = (f32[1,16,128]{2,1,0:T(8,128)S(1)}, f32[1,16,128]{2,1,0:T(8,128)S(1)}, u32[]{:S(2)}, u32[]{:S(2)}) collective-permute-start(f32[1,16,128]{2,1,0:T(8,128)S(1)} %get-tuple-element.47), channel_id=1, source_target_pairs={{0,8},{8,16},{16,24},{1,9},{9,17},{17,25},{2,10},{10,18},{18,26},{... | collective-permute-start | bytes 24584 | tf_op jit(solution)/shard_map/ppermute | solution.py:16
  65.9 4.8 %collective-permute-start.11 = (f32[10,1,128]{2,1,0:T(1,128)S(1)}, f32[10,1,128]{2,1,0:T(1,128)S(1)}, u32[]{:S(2)}, u32[]{:S(2)}) collective-permute-start(f32[10,1,128]{2,1,0:T(1,128)S(1)} %get-tuple-element.40), channel_id=1, source_target_pairs={{0,2},{2,4},{4,6},{1,3},{3,5},{5,7},{8,10},{10,12},{12,14},{9,11},... | collective-permute-start | bytes 15368 | tf_op jit(solution)/shard_map/ppermute | solution.py:16
  72.0 4.2 %collective-permute-done.12 = f32[10,1,128]{2,1,0:T(1,128)S(1)} collective-permute-done((f32[10,1,128]{2,1,0:T(1,128)S(1)}, f32[10,1,128]{2,1,0:T(1,128)S(1)}, u32[]{:S(2)}, u32[]{:S(2)}) %collective-permute-start.12) | collective-permute-done | bytes 5152 | tf_op jit(solution)/shard_map/ppermute | solution.py:19
  79.3 5.5 %reshape.225 = f32[4,2,8,2,64,2]{5,4,3,2,1,0:T(8,128)} reshape(f32[8,16,128]{2,1,0:T(8,128)S(1)} %get-tuple-element.23) | data formatting | bytes 131072 | tf_op jit(solution)/shard_map/reshape | solution.py:48
  84.8 5.5 %reshape.223 = f32[4,2,8,2,64,2]{5,4,3,2,1,0:T(8,128)} reshape(f32[8,16,128]{2,1,0:T(8,128)S(1)} %get-tuple-element.22) | data formatting | bytes 131072 | tf_op jit(solution)/shard_map/reshape | solution.py:48
  90.3 2.8 reduce_sum.350
  93.8 2.8 reduce_sum.348
  96.7 5.5 %reshape.221 = f32[4,2,8,2,64,2]{5,4,3,2,1,0:T(8,128)} reshape(f32[8,16,128]{2,1,0:T(8,128)S(1)} %get-tuple-element.46) | data formatting | bytes 131072 | tf_op jit(solution)/shard_map/reshape | solution.py:48
  102.2 2.8 reduce_sum.346
  105.2 5.5 %reshape.219 = f32[4,2,8,2,64,2]{5,4,3,2,1,0:T(8,128)} reshape(f32[8,16,128]{2,1,0:T(8,128)S(1)} %fusion.18) | data formatting | bytes 131072 | tf_op jit(solution)/shard_map/reshape | solution.py:48
  110.7 2.5 reduce_sum.344
  113.3 4.2 %collective-permute-start.15 = (f32[1,8,64]{2,1,0:T(8,128)S(1)}, f32[1,8,64]{2,1,0:T(8,128)S(1)}, u32[]{:S(2)}, u32[]{:S(2)}) collective-permute-start(f32[1,8,64]{2,1,0:T(8,128)S(1)} %get-tuple-element.73), channel_id=1, source_target_pairs={{0,8},{8,16},{16,24},{1,9},{9,17},{17,25},{2,10},{10,18},{18,26},{... | collective-permute-start | bytes 6152 | tf_op jit(solution)/shard_map/ppermute | solution.py:16
  119.0 4.0 %collective-permute-done.16 = f32[1,8,64]{2,1,0:T(8,128)S(1)} collective-permute-done((f32[1,8,64]{2,1,0:T(8,128)S(1)}, f32[1,8,64]{2,1,0:T(8,128)S(1)}, u32[]{:S(2)}, u32[]{:S(2)}) %collective-permute-start.16) | collective-permute-done | bytes 2080 | tf_op jit(solution)/shard_map/ppermute | solution.py:19
  123.0 2.8 collective-permute-start.17
  127.1 4.2 %collective-permute-done.18 = f32[6,1,64]{2,1,0:T(1,128)S(1)} collective-permute-done((f32[6,1,64]{2,1,0:T(1,128)S(1)}, f32[6,1,64]{2,1,0:T(1,128)S(1)}, u32[]{:S(2)}, u32[]{:S(2)}) %collective-permute-start.18) | collective-permute-done | bytes 1568 | tf_op jit(solution)/shard_map/ppermute | solution.py:19
  135.9 3.5 %collective-permute-start.21 = (f32[1,8,64]{2,1,0:T(8,128)S(1)}, f32[1,8,64]{2,1,0:T(8,128)S(1)}, u32[]{:S(2)}, u32[]{:S(2)}) collective-permute-start(f32[1,8,64]{2,1,0:T(8,128)S(1)} %get-tuple-element.71), channel_id=1, source_target_pairs={{0,8},{8,16},{16,24},{1,9},{9,17},{17,25},{2,10},{10,18},{18,26},{... | collective-permute-start | bytes 6152 | tf_op jit(solution)/shard_map/ppermute | solution.py:16
  141.4 3.5 %collective-permute-done.22 = f32[1,8,64]{2,1,0:T(8,128)S(1)} collective-permute-done((f32[1,8,64]{2,1,0:T(8,128)S(1)}, f32[1,8,64]{2,1,0:T(8,128)S(1)}, u32[]{:S(2)}, u32[]{:S(2)}) %collective-permute-start.22) | collective-permute-done | bytes 2080 | tf_op jit(solution)/shard_map/ppermute | solution.py:19
  144.9 2.8 collective-permute-start.23
  149.9 3.4 %collective-permute-done.24 = f32[6,1,64]{2,1,0:T(1,128)S(1)} collective-permute-done((f32[6,1,64]{2,1,0:T(1,128)S(1)}, f32[6,1,64]{2,1,0:T(1,128)S(1)}, u32[]{:S(2)}, u32[]{:S(2)}) %collective-permute-start.24) | collective-permute-done | bytes 1568 | tf_op jit(solution)/shard_map/ppermute | solution.py:19
  158.5 3.5 %collective-permute-start.27 = (f32[1,4,32]{2,1,0:T(4,128)S(1)}, f32[1,4,32]{2,1,0:T(4,128)S(1)}, u32[]{:S(2)}, u32[]{:S(2)}) collective-permute-start(f32[1,4,32]{2,1,0:T(4,128)S(1)} %get-tuple-element.85), channel_id=1, source_target_pairs={{0,8},{8,16},{16,24},{1,9},{9,17},{17,25},{2,10},{10,18},{18,26},{... | collective-permute-start | bytes 1544 | tf_op jit(solution)/shard_map/ppermute | solution.py:16
  163.5 4.0 %collective-permute-done.28 = f32[1,4,32]{2,1,0:T(4,128)S(1)} collective-permute-done((f32[1,4,32]{2,1,0:T(4,128)S(1)}, f32[1,4,32]{2,1,0:T(4,128)S(1)}, u32[]{:S(2)}, u32[]{:S(2)}) %collective-permute-start.28) | collective-permute-done | bytes 544 | tf_op jit(solution)/shard_map/ppermute | solution.py:19
  167.5 2.8 collective-permute-start.29
  171.7 4.2 %collective-permute-done.30 = f32[4,1,32]{2,1,0:T(1,128)S(1)} collective-permute-done((f32[4,1,32]{2,1,0:T(1,128)S(1)}, f32[4,1,32]{2,1,0:T(1,128)S(1)}, u32[]{:S(2)}, u32[]{:S(2)}) %collective-permute-start.30) | collective-permute-done | bytes 544 | tf_op jit(solution)/shard_map/ppermute | solution.py:19
  183.8 4.0 %collective-permute-done.34 = f32[1,4,32]{2,1,0:T(4,128)S(1)} collective-permute-done((f32[1,4,32]{2,1,0:T(4,128)S(1)}, f32[1,4,32]{2,1,0:T(4,128)S(1)}, u32[]{:S(2)}, u32[]{:S(2)}) %collective-permute-start.34) | collective-permute-done | bytes 544 | tf_op jit(solution)/shard_map/ppermute | solution.py:19
  187.8 2.8 collective-permute-start.35
  192.1 4.0 %collective-permute-done.36 = f32[4,1,32]{2,1,0:T(1,128)S(1)} collective-permute-done((f32[4,1,32]{2,1,0:T(1,128)S(1)}, f32[4,1,32]{2,1,0:T(1,128)S(1)}, u32[]{:S(2)}, u32[]{:S(2)}) %collective-permute-start.36) | collective-permute-done | bytes 544 | tf_op jit(solution)/shard_map/ppermute | solution.py:19
  200.9 38.1 %all-gather = f32[224,1,2,16]{3,2,1,0:T(2,128)S(1)} all-gather(f32[7,1,2,16]{3,2,1,0:T(2,128)S(1)} %constant_dynamic-update-slice_fusion), channel_id=2, replica_groups=mesh['gx'=4,'gy'=4,'gz'=2] {'gx','gy','gz'}, dimensions={0}, use_global_device_ids=true | all-gather | bytes 29568 | tf_op jit(solution)/shard_map/all_gather | solution.py:104
  266.2 4.2 %collective-permute-done.40 = f32[1,4,32]{2,1,0:T(4,128)S(1)} collective-permute-done((f32[1,4,32]{2,1,0:T(4,128)S(1)}, f32[1,4,32]{2,1,0:T(4,128)S(1)}, u32[]{:S(2)}, u32[]{:S(2)}) %collective-permute-start.40) | collective-permute-done | bytes 544 | tf_op jit(solution)/shard_map/ppermute | solution.py:19
  270.4 3.0 collective-permute-start.41
  274.7 4.2 %collective-permute-done.42 = f32[4,1,32]{2,1,0:T(1,128)S(1)} collective-permute-done((f32[4,1,32]{2,1,0:T(1,128)S(1)}, f32[4,1,32]{2,1,0:T(1,128)S(1)}, u32[]{:S(2)}, u32[]{:S(2)}) %collective-permute-start.42) | collective-permute-done | bytes 544 | tf_op jit(solution)/shard_map/ppermute | solution.py:19
  286.8 4.2 %collective-permute-done.46 = f32[1,8,64]{2,1,0:T(8,128)S(1)} collective-permute-done((f32[1,8,64]{2,1,0:T(8,128)S(1)}, f32[1,8,64]{2,1,0:T(8,128)S(1)}, u32[]{:S(2)}, u32[]{:S(2)}) %collective-permute-start.46) | collective-permute-done | bytes 2080 | tf_op jit(solution)/shard_map/ppermute | solution.py:19
  291.0 2.8 collective-permute-start.47
  295.2 4.2 %collective-permute-done.48 = f32[6,1,64]{2,1,0:T(1,128)S(1)} collective-permute-done((f32[6,1,64]{2,1,0:T(1,128)S(1)}, f32[6,1,64]{2,1,0:T(1,128)S(1)}, u32[]{:S(2)}, u32[]{:S(2)}) %collective-permute-start.48) | collective-permute-done | bytes 1568 | tf_op jit(solution)/shard_map/ppermute | solution.py:19
  306.5 4.0 %reshape.229 = f32[8,16,128]{2,1,0:T(8,128)S(1)} reshape(f32[4,2,8,2,64,2]{5,4,3,2,1,0:T(8,128)} %broadcast_in_dim.33) | data formatting | bytes 131072 | tf_op jit(solution)/shard_map/reshape | solution.py:75
  310.5 3.9 %collective-permute-start.51 = (f32[1,16,128]{2,1,0:T(8,128)S(1)}, f32[1,16,128]{2,1,0:T(8,128)S(1)}, u32[]{:S(2)}, u32[]{:S(2)}) collective-permute-start(f32[1,16,128]{2,1,0:T(8,128)S(1)} %get-tuple-element.44), channel_id=1, source_target_pairs={{0,8},{8,16},{16,24},{1,9},{9,17},{17,25},{2,10},{10,18},{18,26},{... | collective-permute-start | bytes 24584 | tf_op jit(solution)/shard_map/ppermute | solution.py:16
  315.7 4.2 %collective-permute-done.52 = f32[1,16,128]{2,1,0:T(8,128)S(1)} collective-permute-done((f32[1,16,128]{2,1,0:T(8,128)S(1)}, f32[1,16,128]{2,1,0:T(8,128)S(1)}, u32[]{:S(2)}, u32[]{:S(2)}) %collective-permute-start.52) | collective-permute-done | bytes 8224 | tf_op jit(solution)/shard_map/ppermute | solution.py:19
  320.0 4.5 %collective-permute-start.53 = (f32[10,1,128]{2,1,0:T(1,128)S(1)}, f32[10,1,128]{2,1,0:T(1,128)S(1)}, u32[]{:S(2)}, u32[]{:S(2)}) collective-permute-start(f32[10,1,128]{2,1,0:T(1,128)S(1)} %get-tuple-element.38), channel_id=1, source_target_pairs={{0,2},{2,4},{4,6},{1,3},{3,5},{5,7},{8,10},{10,12},{12,14},{9,11},... | collective-permute-start | bytes 15368 | tf_op jit(solution)/shard_map/ppermute | solution.py:16
  325.8 4.2 %collective-permute-done.54 = f32[10,1,128]{2,1,0:T(1,128)S(1)} collective-permute-done((f32[10,1,128]{2,1,0:T(1,128)S(1)}, f32[10,1,128]{2,1,0:T(1,128)S(1)}, u32[]{:S(2)}, u32[]{:S(2)}) %collective-permute-start.54) | collective-permute-done | bytes 5152 | tf_op jit(solution)/shard_map/ppermute | solution.py:19
  (247 shorter events, 93.8 us)
Async XLA Ops:
  0.7 30.9 %collective-permute-start = (f32[1,16,128]{2,1,0:T(8,128)S(1)}, f32[1,16,128]{2,1,0:T(8,128)S(1)}, u32[]{:S(2)}, u32[]{:S(2)}) collective-permute-start(f32[1,16,128]{2,1,0:T(8,128)S(1)} %slice.587), channel_id=1, source_target_pairs={{8,0},{16,8},{24,16},{9,1},{17,9},{25,17},{10,2},{18,10},{26,18},{... | collective-permute-start | bytes 24584 | tf_op jit(solution)/shard_map/ppermute | solution.py:27
  2.0 29.6 %collective-permute-start.2 = (f32[8,16,1]{2,1,0:T(8,128)}, f32[8,16,1]{2,1,0:T(8,128)S(1)}, u32[]{:S(2)}, u32[]{:S(2)}) collective-permute-start(f32[8,16,1]{2,1,0:T(8,128)} %bitcast.288), channel_id=1, source_target_pairs={{1,0},{3,2},{5,4},{7,6},{9,8},{11,10},{13,12},{15,14},{17,16},{19,... | collective-permute-start | bytes 1544 | tf_op jit(solution)/shard_map/ppermute | solution.py:27
  4.1 27.6 %collective-permute-start.1 = (f32[8,1,128]{2,1,0:T(1,128)S(1)}, f32[8,1,128]{2,1,0:T(1,128)S(1)}, u32[]{:S(2)}, u32[]{:S(2)}) collective-permute-start(f32[8,1,128]{2,1,0:T(1,128)S(1)} %slice.589), channel_id=1, source_target_pairs={{2,0},{4,2},{6,4},{3,1},{5,3},{7,5},{10,8},{12,10},{14,12},{11,9},... | collective-permute-start | bytes 12296 | tf_op jit(solution)/shard_map/ppermute | solution.py:27
  31.8 7.6 %collective-permute-start.3 = (f32[1,16,128]{2,1,0:T(8,128)S(1)}, f32[1,16,128]{2,1,0:T(8,128)S(1)}, u32[]{:S(2)}, u32[]{:S(2)}) collective-permute-start(f32[1,16,128]{2,1,0:T(8,128)S(1)} %get-tuple-element.49), channel_id=1, source_target_pairs={{0,8},{8,16},{16,24},{1,9},{9,17},{17,25},{2,10},{10,18},{18,26},{... | collective-permute-start | bytes 24584 | tf_op jit(solution)/shard_map/ppermute | solution.py:16
  37.4 5.5 %collective-permute-start.4 = (f32[1,16,128]{2,1,0:T(8,128)S(1)}, f32[1,16,128]{2,1,0:T(8,128)S(1)}, u32[]{:S(2)}, u32[]{:S(2)}) collective-permute-start(f32[1,16,128]{2,1,0:T(8,128)S(1)} %get-tuple-element.50), channel_id=1, source_target_pairs={{8,0},{16,8},{24,16},{9,1},{17,9},{25,17},{10,2},{18,10},{26,18},{... | collective-permute-start | bytes 24584 | tf_op jit(solution)/shard_map/ppermute | solution.py:19
  43.0 6.6 %collective-permute-start.5 = (f32[10,1,128]{2,1,0:T(1,128)S(1)}, f32[10,1,128]{2,1,0:T(1,128)S(1)}, u32[]{:S(2)}, u32[]{:S(2)}) collective-permute-start(f32[10,1,128]{2,1,0:T(1,128)S(1)} %get-tuple-element.42), channel_id=1, source_target_pairs={{0,2},{2,4},{4,6},{1,3},{3,5},{5,7},{8,10},{10,12},{12,14},{9,11},... | collective-permute-start | bytes 15368 | tf_op jit(solution)/shard_map/ppermute | solution.py:16
  47.5 6.3 %collective-permute-start.6 = (f32[10,1,128]{2,1,0:T(1,128)S(1)}, f32[10,1,128]{2,1,0:T(1,128)S(1)}, u32[]{:S(2)}, u32[]{:S(2)}) collective-permute-start(f32[10,1,128]{2,1,0:T(1,128)S(1)} %get-tuple-element.43), channel_id=1, source_target_pairs={{2,0},{4,2},{6,4},{3,1},{5,3},{7,5},{10,8},{12,10},{14,12},{11,9},... | collective-permute-start | bytes 15368 | tf_op jit(solution)/shard_map/ppermute | solution.py:19
  55.3 3.2 collective-permute-start.8
  58.7 6.6 %collective-permute-start.10 = (f32[1,16,128]{2,1,0:T(8,128)S(1)}, f32[1,16,128]{2,1,0:T(8,128)S(1)}, u32[]{:S(2)}, u32[]{:S(2)}) collective-permute-start(f32[1,16,128]{2,1,0:T(8,128)S(1)} %get-tuple-element.48), channel_id=1, source_target_pairs={{8,0},{16,8},{24,16},{9,1},{17,9},{25,17},{10,2},{18,10},{26,18},{... | collective-permute-start | bytes 24584 | tf_op jit(solution)/shard_map/ppermute | solution.py:19
  60.0 5.9 %collective-permute-start.9 = (f32[1,16,128]{2,1,0:T(8,128)S(1)}, f32[1,16,128]{2,1,0:T(8,128)S(1)}, u32[]{:S(2)}, u32[]{:S(2)}) collective-permute-start(f32[1,16,128]{2,1,0:T(8,128)S(1)} %get-tuple-element.47), channel_id=1, source_target_pairs={{0,8},{8,16},{16,24},{1,9},{9,17},{17,25},{2,10},{10,18},{18,26},{... | collective-permute-start | bytes 24584 | tf_op jit(solution)/shard_map/ppermute | solution.py:16
  65.9 6.1 %collective-permute-start.11 = (f32[10,1,128]{2,1,0:T(1,128)S(1)}, f32[10,1,128]{2,1,0:T(1,128)S(1)}, u32[]{:S(2)}, u32[]{:S(2)}) collective-permute-start(f32[10,1,128]{2,1,0:T(1,128)S(1)} %get-tuple-element.40), channel_id=1, source_target_pairs={{0,2},{2,4},{4,6},{1,3},{3,5},{5,7},{8,10},{10,12},{12,14},{9,11},... | collective-permute-start | bytes 15368 | tf_op jit(solution)/shard_map/ppermute | solution.py:16
  70.7 5.5 %collective-permute-start.12 = (f32[10,1,128]{2,1,0:T(1,128)S(1)}, f32[10,1,128]{2,1,0:T(1,128)S(1)}, u32[]{:S(2)}, u32[]{:S(2)}) collective-permute-start(f32[10,1,128]{2,1,0:T(1,128)S(1)} %get-tuple-element.41), channel_id=1, source_target_pairs={{2,0},{4,2},{6,4},{3,1},{5,3},{7,5},{10,8},{12,10},{14,12},{11,9},... | collective-permute-start | bytes 15368 | tf_op jit(solution)/shard_map/ppermute | solution.py:19
  76.3 28.7 %collective-permute-start.13 = (f32[10,18,1]{2,1,0:T(8,128)S(1)}, f32[10,18,1]{2,1,0:T(8,128)S(1)}, u32[]{:S(2)}, u32[]{:S(2)}) collective-permute-start(f32[10,18,1]{2,1,0:T(8,128)S(1)} %get-tuple-element.34), channel_id=1, source_target_pairs={{0,1},{2,3},{4,5},{6,7},{8,9},{10,11},{12,13},{14,15},{16,17},{18,... | collective-permute-start | bytes 2168 | tf_op jit(solution)/shard_map/ppermute | solution.py:16
  77.6 27.4 %collective-permute-start.14 = (f32[10,18,1]{2,1,0:T(8,128)S(1)}, f32[10,18,1]{2,1,0:T(8,128)S(1)}, u32[]{:S(2)}, u32[]{:S(2)}) collective-permute-start(f32[10,18,1]{2,1,0:T(8,128)S(1)} %get-tuple-element.35), channel_id=1, source_target_pairs={{1,0},{3,2},{5,4},{7,6},{9,8},{11,10},{13,12},{15,14},{17,16},{19,... | collective-permute-start | bytes 2168 | tf_op jit(solution)/shard_map/ppermute | solution.py:19
  113.3 5.7 %collective-permute-start.15 = (f32[1,8,64]{2,1,0:T(8,128)S(1)}, f32[1,8,64]{2,1,0:T(8,128)S(1)}, u32[]{:S(2)}, u32[]{:S(2)}) collective-permute-start(f32[1,8,64]{2,1,0:T(8,128)S(1)} %get-tuple-element.73), channel_id=1, source_target_pairs={{0,8},{8,16},{16,24},{1,9},{9,17},{17,25},{2,10},{10,18},{18,26},{... | collective-permute-start | bytes 6152 | tf_op jit(solution)/shard_map/ppermute | solution.py:16
  117.5 5.5 %collective-permute-start.16 = (f32[1,8,64]{2,1,0:T(8,128)S(1)}, f32[1,8,64]{2,1,0:T(8,128)S(1)}, u32[]{:S(2)}, u32[]{:S(2)}) collective-permute-start(f32[1,8,64]{2,1,0:T(8,128)S(1)} %get-tuple-element.74), channel_id=1, source_target_pairs={{8,0},{16,8},{24,16},{9,1},{17,9},{25,17},{10,2},{18,10},{26,18},{... | collective-permute-start | bytes 6152 | tf_op jit(solution)/shard_map/ppermute | solution.py:19
  123.0 4.1 %collective-permute-start.17 = (f32[6,1,64]{2,1,0:T(1,128)S(1)}, f32[6,1,64]{2,1,0:T(1,128)S(1)}, u32[]{:S(2)}, u32[]{:S(2)}) collective-permute-start(f32[6,1,64]{2,1,0:T(1,128)S(1)} %get-tuple-element.61), channel_id=1, source_target_pairs={{0,2},{2,4},{4,6},{1,3},{3,5},{5,7},{8,10},{10,12},{12,14},{9,11},... | collective-permute-start | bytes 4616 | tf_op jit(solution)/shard_map/ppermute | solution.py:16
  125.8 5.5 %collective-permute-start.18 = (f32[6,1,64]{2,1,0:T(1,128)S(1)}, f32[6,1,64]{2,1,0:T(1,128)S(1)}, u32[]{:S(2)}, u32[]{:S(2)}) collective-permute-start(f32[6,1,64]{2,1,0:T(1,128)S(1)} %get-tuple-element.62), channel_id=1, source_target_pairs={{2,0},{4,2},{6,4},{3,1},{5,3},{7,5},{10,8},{12,10},{14,12},{11,9},... | collective-permute-start | bytes 4616 | tf_op jit(solution)/shard_map/ppermute | solution.py:19
  132.7 3.1 collective-permute-start.20
  135.9 5.5 %collective-permute-start.21 = (f32[1,8,64]{2,1,0:T(8,128)S(1)}, f32[1,8,64]{2,1,0:T(8,128)S(1)}, u32[]{:S(2)}, u32[]{:S(2)}) collective-permute-start(f32[1,8,64]{2,1,0:T(8,128)S(1)} %get-tuple-element.71), channel_id=1, source_target_pairs={{0,8},{8,16},{16,24},{1,9},{9,17},{17,25},{2,10},{10,18},{18,26},{... | collective-permute-start | bytes 6152 | tf_op jit(solution)/shard_map/ppermute | solution.py:16
  139.4 5.5 %collective-permute-start.22 = (f32[1,8,64]{2,1,0:T(8,128)S(1)}, f32[1,8,64]{2,1,0:T(8,128)S(1)}, u32[]{:S(2)}, u32[]{:S(2)}) collective-permute-start(f32[1,8,64]{2,1,0:T(8,128)S(1)} %get-tuple-element.72), channel_id=1, source_target_pairs={{8,0},{16,8},{24,16},{9,1},{17,9},{25,17},{10,2},{18,10},{26,18},{... | collective-permute-start | bytes 6152 | tf_op jit(solution)/shard_map/ppermute | solution.py:19
  144.9 4.9 %collective-permute-start.23 = (f32[6,1,64]{2,1,0:T(1,128)S(1)}, f32[6,1,64]{2,1,0:T(1,128)S(1)}, u32[]{:S(2)}, u32[]{:S(2)}) collective-permute-start(f32[6,1,64]{2,1,0:T(1,128)S(1)} %get-tuple-element.59), channel_id=1, source_target_pairs={{0,2},{2,4},{4,6},{1,3},{3,5},{5,7},{8,10},{10,12},{12,14},{9,11},... | collective-permute-start | bytes 4616 | tf_op jit(solution)/shard_map/ppermute | solution.py:16
  147.7 5.5 %collective-permute-start.24 = (f32[6,1,64]{2,1,0:T(1,128)S(1)}, f32[6,1,64]{2,1,0:T(1,128)S(1)}, u32[]{:S(2)}, u32[]{:S(2)}) collective-permute-start(f32[6,1,64]{2,1,0:T(1,128)S(1)} %get-tuple-element.60), channel_id=1, source_target_pairs={{2,0},{4,2},{6,4},{3,1},{5,3},{7,5},{10,8},{12,10},{14,12},{11,9},... | collective-permute-start | bytes 4616 | tf_op jit(solution)/shard_map/ppermute | solution.py:19
  153.3 3.3 collective-permute-start.25
  154.6 3.1 collective-permute-start.26
  158.5 5.0 %collective-permute-start.27 = (f32[1,4,32]{2,1,0:T(4,128)S(1)}, f32[1,4,32]{2,1,0:T(4,128)S(1)}, u32[]{:S(2)}, u32[]{:S(2)}) collective-permute-start(f32[1,4,32]{2,1,0:T(4,128)S(1)} %get-tuple-element.85), channel_id=1, source_target_pairs={{0,8},{8,16},{16,24},{1,9},{9,17},{17,25},{2,10},{10,18},{18,26},{... | collective-permute-start | bytes 1544 | tf_op jit(solution)/shard_map/ppermute | solution.py:16
  162.0 5.5 %collective-permute-start.28 = (f32[1,4,32]{2,1,0:T(4,128)S(1)}, f32[1,4,32]{2,1,0:T(4,128)S(1)}, u32[]{:S(2)}, u32[]{:S(2)}) collective-permute-start(f32[1,4,32]{2,1,0:T(4,128)S(1)} %get-tuple-element.86), channel_id=1, source_target_pairs={{8,0},{16,8},{24,16},{9,1},{17,9},{25,17},{10,2},{18,10},{26,18},{... | collective-permute-start | bytes 1544 | tf_op jit(solution)/shard_map/ppermute | solution.py:19
  167.5 4.1 %collective-permute-start.29 = (f32[4,1,32]{2,1,0:T(1,128)S(1)}, f32[4,1,32]{2,1,0:T(1,128)S(1)}, u32[]{:S(2)}, u32[]{:S(2)}) collective-permute-start(f32[4,1,32]{2,1,0:T(1,128)S(1)} %get-tuple-element.79), channel_id=1, source_target_pairs={{0,2},{2,4},{4,6},{1,3},{3,5},{5,7},{8,10},{10,12},{12,14},{9,11},... | collective-permute-start | bytes 1544 | tf_op jit(solution)/shard_map/ppermute | solution.py:16
  170.3 5.5 %collective-permute-start.30 = (f32[4,1,32]{2,1,0:T(1,128)S(1)}, f32[4,1,32]{2,1,0:T(1,128)S(1)}, u32[]{:S(2)}, u32[]{:S(2)}) collective-permute-start(f32[4,1,32]{2,1,0:T(1,128)S(1)} %get-tuple-element.80), channel_id=1, source_target_pairs={{2,0},{4,2},{6,4},{3,1},{5,3},{7,5},{10,8},{12,10},{14,12},{11,9},... | collective-permute-start | bytes 1544 | tf_op jit(solution)/shard_map/ppermute | solution.py:19
  177.2 3.1 collective-permute-start.32
  180.4 3.4 %collective-permute-start.33 = (f32[1,4,32]{2,1,0:T(4,128)S(1)}, f32[1,4,32]{2,1,0:T(4,128)S(1)}, u32[]{:S(2)}, u32[]{:S(2)}) collective-permute-start(f32[1,4,32]{2,1,0:T(4,128)S(1)} %get-tuple-element.83), channel_id=1, source_target_pairs={{0,8},{8,16},{16,24},{1,9},{9,17},{17,25},{2,10},{10,18},{18,26},{... | collective-permute-start | bytes 1544 | tf_op jit(solution)/shard_map/ppermute | solution.py:16
  182.3 5.5 %collective-permute-start.34 = (f32[1,4,32]{2,1,0:T(4,128)S(1)}, f32[1,4,32]{2,1,0:T(4,128)S(1)}, u32[]{:S(2)}, u32[]{:S(2)}) collective-permute-start(f32[1,4,32]{2,1,0:T(4,128)S(1)} %get-tuple-element.84), channel_id=1, source_target_pairs={{8,0},{16,8},{24,16},{9,1},{17,9},{25,17},{10,2},{18,10},{26,18},{... | collective-permute-start | bytes 1544 | tf_op jit(solution)/shard_map/ppermute | solution.py:19
  187.8 4.3 %collective-permute-start.35 = (f32[4,1,32]{2,1,0:T(1,128)S(1)}, f32[4,1,32]{2,1,0:T(1,128)S(1)}, u32[]{:S(2)}, u32[]{:S(2)}) collective-permute-start(f32[4,1,32]{2,1,0:T(1,128)S(1)} %get-tuple-element.77), channel_id=1, source_target_pairs={{0,2},{2,4},{4,6},{1,3},{3,5},{5,7},{8,10},{10,12},{12,14},{9,11},... | collective-permute-start | bytes 1544 | tf_op jit(solution)/shard_map/ppermute | solution.py:16
  190.6 5.5 %collective-permute-start.36 = (f32[4,1,32]{2,1,0:T(1,128)S(1)}, f32[4,1,32]{2,1,0:T(1,128)S(1)}, u32[]{:S(2)}, u32[]{:S(2)}) collective-permute-start(f32[4,1,32]{2,1,0:T(1,128)S(1)} %get-tuple-element.78), channel_id=1, source_target_pairs={{2,0},{4,2},{6,4},{3,1},{5,3},{7,5},{10,8},{12,10},{14,12},{11,9},... | collective-permute-start | bytes 1544 | tf_op jit(solution)/shard_map/ppermute | solution.py:19
  197.5 3.1 collective-permute-start.38
  264.9 5.5 %collective-permute-start.40 = (f32[1,4,32]{2,1,0:T(4,128)S(1)}, f32[1,4,32]{2,1,0:T(4,128)S(1)}, u32[]{:S(2)}, u32[]{:S(2)}) collective-permute-start(f32[1,4,32]{2,1,0:T(4,128)S(1)} %get-tuple-element.82), channel_id=1, source_target_pairs={{8,0},{16,8},{24,16},{9,1},{17,9},{25,17},{10,2},{18,10},{26,18},{... | collective-permute-start | bytes 1544 | tf_op jit(solution)/shard_map/ppermute | solution.py:19
  270.4 4.3 %collective-permute-start.41 = (f32[4,1,32]{2,1,0:T(1,128)S(1)}, f32[4,1,32]{2,1,0:T(1,128)S(1)}, u32[]{:S(2)}, u32[]{:S(2)}) collective-permute-start(f32[4,1,32]{2,1,0:T(1,128)S(1)} %get-tuple-element.75), channel_id=1, source_target_pairs={{0,2},{2,4},{4,6},{1,3},{3,5},{5,7},{8,10},{10,12},{12,14},{9,11},... | collective-permute-start | bytes 1544 | tf_op jit(solution)/shard_map/ppermute | solution.py:16
  273.4 5.5 %collective-permute-start.42 = (f32[4,1,32]{2,1,0:T(1,128)S(1)}, f32[4,1,32]{2,1,0:T(1,128)S(1)}, u32[]{:S(2)}, u32[]{:S(2)}) collective-permute-start(f32[4,1,32]{2,1,0:T(1,128)S(1)} %get-tuple-element.76), channel_id=1, source_target_pairs={{2,0},{4,2},{6,4},{3,1},{5,3},{7,5},{10,8},{12,10},{14,12},{11,9},... | collective-permute-start | bytes 1544 | tf_op jit(solution)/shard_map/ppermute | solution.py:19
  280.3 3.1 collective-permute-start.44
  285.5 5.5 %collective-permute-start.46 = (f32[1,8,64]{2,1,0:T(8,128)S(1)}, f32[1,8,64]{2,1,0:T(8,128)S(1)}, u32[]{:S(2)}, u32[]{:S(2)}) collective-permute-start(f32[1,8,64]{2,1,0:T(8,128)S(1)} %get-tuple-element.64), channel_id=1, source_target_pairs={{8,0},{16,8},{24,16},{9,1},{17,9},{25,17},{10,2},{18,10},{26,18},{... | collective-permute-start | bytes 6152 | tf_op jit(solution)/shard_map/ppermute | solution.py:19
  291.0 4.1 %collective-permute-start.47 = (f32[6,1,64]{2,1,0:T(1,128)S(1)}, f32[6,1,64]{2,1,0:T(1,128)S(1)}, u32[]{:S(2)}, u32[]{:S(2)}) collective-permute-start(f32[6,1,64]{2,1,0:T(1,128)S(1)} %get-tuple-element.57), channel_id=1, source_target_pairs={{0,2},{2,4},{4,6},{1,3},{3,5},{5,7},{8,10},{10,12},{12,14},{9,11},... | collective-permute-start | bytes 4616 | tf_op jit(solution)/shard_map/ppermute | solution.py:16
  293.9 5.5 %collective-permute-start.48 = (f32[6,1,64]{2,1,0:T(1,128)S(1)}, f32[6,1,64]{2,1,0:T(1,128)S(1)}, u32[]{:S(2)}, u32[]{:S(2)}) collective-permute-start(f32[6,1,64]{2,1,0:T(1,128)S(1)} %get-tuple-element.58), channel_id=1, source_target_pairs={{2,0},{4,2},{6,4},{3,1},{5,3},{7,5},{10,8},{12,10},{14,12},{11,9},... | collective-permute-start | bytes 4616 | tf_op jit(solution)/shard_map/ppermute | solution.py:19
  300.7 3.1 collective-permute-start.50
  310.5 5.2 %collective-permute-start.51 = (f32[1,16,128]{2,1,0:T(8,128)S(1)}, f32[1,16,128]{2,1,0:T(8,128)S(1)}, u32[]{:S(2)}, u32[]{:S(2)}) collective-permute-start(f32[1,16,128]{2,1,0:T(8,128)S(1)} %get-tuple-element.44), channel_id=1, source_target_pairs={{0,8},{8,16},{16,24},{1,9},{9,17},{17,25},{2,10},{10,18},{18,26},{... | collective-permute-start | bytes 24584 | tf_op jit(solution)/shard_map/ppermute | solution.py:16
  314.4 5.5 %collective-permute-start.52 = (f32[1,16,128]{2,1,0:T(8,128)S(1)}, f32[1,16,128]{2,1,0:T(8,128)S(1)}, u32[]{:S(2)}, u32[]{:S(2)}) collective-permute-start(f32[1,16,128]{2,1,0:T(8,128)S(1)} %get-tuple-element.45), channel_id=1, source_target_pairs={{8,0},{16,8},{24,16},{9,1},{17,9},{25,17},{10,2},{18,10},{26,18},{... | collective-permute-start | bytes 24584 | tf_op jit(solution)/shard_map/ppermute | solution.py:19
  320.0 5.9 %collective-permute-start.53 = (f32[10,1,128]{2,1,0:T(1,128)S(1)}, f32[10,1,128]{2,1,0:T(1,128)S(1)}, u32[]{:S(2)}, u32[]{:S(2)}) collective-permute-start(f32[10,1,128]{2,1,0:T(1,128)S(1)} %get-tuple-element.38), channel_id=1, source_target_pairs={{0,2},{2,4},{4,6},{1,3},{3,5},{5,7},{8,10},{10,12},{12,14},{9,11},... | collective-permute-start | bytes 15368 | tf_op jit(solution)/shard_map/ppermute | solution.py:16
  324.5 5.5 %collective-permute-start.54 = (f32[10,1,128]{2,1,0:T(1,128)S(1)}, f32[10,1,128]{2,1,0:T(1,128)S(1)}, u32[]{:S(2)}, u32[]{:S(2)}) collective-permute-start(f32[10,1,128]{2,1,0:T(1,128)S(1)} %get-tuple-element.39), channel_id=1, source_target_pairs={{2,0},{4,2},{6,4},{3,1},{5,3},{7,5},{10,8},{12,10},{14,12},{11,9},... | collective-permute-start | bytes 15368 | tf_op jit(solution)/shard_map/ppermute | solution.py:19
  331.4 3.2 collective-permute-start.56
  (13 other events, 56.1 us)
where the time goes:
time: 338 us; the launch traced here: 335 us
  starting transfers between devices  112 us (33%)
  waiting for transfers between devices  82.6 us (24%)
  local copies, waits for them, and re-layouts  55.4 us (16%)
  blocking collectives  38.1 us (11%)
  other arithmetic  31.3 us (9%)
  between operations  16.5 us (5%)
    ppermute x27, waiting for transfers between devices, extended(): lax.ppermute(lax.slice_in_dim(block, 0, width, axis=dim), axis, backward)  81.9 us
    ppermute x27, starting transfers between devices, extended(): lax.ppermute(lax.slice_in_dim(block, block.shape[dim] - width, None, axis...  72.6 us
    reshape x8, local copies, waits for them, and re-layouts, blocked(): values.reshape(values.shape[0] // 2, 2, values.shape[1] // 2, 2, values.s...  39.8 us
    all_gather x1, blocking collectives, coarse_solve(): whole = lax.all_gather(stacked, ('gx', 'gy', 'gz'), axis=0, tiled=True)  38.1 us
    ppermute x27, starting transfers between devices, extended(): lax.ppermute(lax.slice_in_dim(block, 0, width, axis=dim), axis, backward)  35.1 us
    reduce_sum x22, other arithmetic, coarse_face(): summed = jnp.sum(blocked(values), axis=others)  18 us
  transfers between devices with their start and end apart: 57, of which 26 were waited for; matrix products, arithmetic and copies ran while one was open for 17% of the time, Pallas kernels for 0%

commit v1 on v0

--- a/solution.py
+++ b/solution.py
@@ -101,7 +101,19 @@
     count_y = lax.axis_size("gy")
     count_z = lax.axis_size("gz")
     stacked = jnp.stack((rhs,) + coefs)[None]
-    whole = lax.all_gather(stacked, ("gx", "gy", "gz"), axis=0, tiled=True)
+    wide_out = lax.axis_size(("gx", "gy", "gz"))
+    known = lax.axis_index(("gx", "gy", "gz"))
+    latest, kept_arr = (wide_out, known)
+    whole, inter = (stacked, 1)
+    while inter < latest:
+        xs_all = []
+        for c in range(latest):
+            xs_all.append((c, c ^ inter))
+        val = lax.ppermute(whole, ("gx", "gy", "gz"), perm=xs_all)
+        z2 = jnp.concatenate([whole, val], 0)
+        t_next = jnp.concatenate([val, whole], axis=0)
+        whole = jnp.where(kept_arr & inter == 0, z2, t_next)
+        inter = 2 * inter
     whole = whole.reshape(count_x, count_y, count_z, 7, part_x, part_y, part_z)
     whole = whole.transpose(3, 0, 4, 1, 5, 2, 6).reshape(
         7, count_x * part_x, count_y * part_y, count_z * part_z

time: 338 us -> 317 us (0.938)
  blocking collectives: 38.1 us -> 0 us
  waiting for transfers between devices: 82.6 us -> 101 us
    all_gather x1 -> x0, blocking collectives: 38.1 us -> none  [coarse_solve(): whole = lax.all_gather(stacked, ('gx', 'gy', 'gz'), axis=0, tiled=True)]
    ppermute x0 -> x5, waiting for transfers between devices: none -> 18.4 us  [coarse_solve(): val = lax.ppermute(whole, ('gx', 'gy', 'gz'), perm=xs_all)]
  transfers between devices with their start and end apart: 57 -> 62, of which waited for: 26 -> 31; matrix products, arithmetic and copies ran while one was open for 17% -> 18% of each run, Pallas kernels for 0% -> 0%
where the time goes in v1:
time: 317 us; the launch traced here: 315 us
  starting transfers between devices  111 us (35%)
  waiting for transfers between devices  101 us (32%)
  local copies, waits for them, and re-layouts  55.4 us (17%)
  other arithmetic  31.6 us (10%)
  between operations  16.6 us (5%)
    ppermute x27, waiting for transfers between devices, extended(): lax.ppermute(lax.slice_in_dim(block, 0, width, axis=dim), axis, backward)  81.6 us
    ppermute x27, starting transfers between devices, extended(): lax.ppermute(lax.slice_in_dim(block, block.shape[dim] - width, None, axis...  70 us
    reshape x8, local copies, waits for them, and re-layouts, blocked(): values.reshape(values.shape[0] // 2, 2, values.shape[1] // 2, 2, values.s...  39.8 us
    ppermute x27, starting transfers between devices, extended(): lax.ppermute(lax.slice_in_dim(block, 0, width, axis=dim), axis, backward)  35.3 us
    ppermute x5, waiting for transfers between devices, coarse_solve(): val = lax.ppermute(whole, ('gx', 'gy', 'gz'), perm=xs_all)  18.4 us
    reduce_sum x22, other arithmetic, coarse_face(): summed = jnp.sum(blocked(values), axis=others)  18 us
  transfers between devices with their start and end apart: 62, of which 31 were waited for; matrix products, arithmetic and copies ran while one was open for 18% of the time, Pallas kernels for 0%

profile of v1, /device:TPU:0, one launch (start us, length us, event | category | flops | bytes accessed | tf_op | source)
XLA Modules:
  0.0 315.1 jit_solution(1506109364347475774)
XLA Ops:
  5.4 6.3 %reshape.692 = f32[4,2,8,2,64,2]{5,4,3,2,1,0:T(8,128)} reshape(f32[8,16,128]{2,1,0:T(8,128)} %param.7) | data formatting | bytes 131072 | tf_op jit(solution)/shard_map/reshape | solution.py:48
  11.7 5.5 %reshape.690 = f32[4,2,8,2,64,2]{5,4,3,2,1,0:T(8,128)} reshape(f32[8,16,128]{2,1,0:T(8,128)S(1)} %copy-done) | data formatting | bytes 131072 | tf_op jit(solution)/shard_map/reshape | solution.py:48
  20.3 2.8 reduce_sum.347
  23.3 5.5 %reshape.688 = f32[4,2,8,2,64,2]{5,4,3,2,1,0:T(8,128)} reshape(f32[8,16,128]{2,1,0:T(8,128)S(1)} %copy-done.2) | data formatting | bytes 131072 | tf_op jit(solution)/shard_map/reshape | solution.py:48
  28.8 2.8 reduce_sum.345
  31.8 5.6 %collective-permute-start.3 = (f32[1,16,128]{2,1,0:T(8,128)S(1)}, f32[1,16,128]{2,1,0:T(8,128)S(1)}, u32[]{:S(2)}, u32[]{:S(2)}) collective-permute-start(f32[1,16,128]{2,1,0:T(8,128)S(1)} %get-tuple-element.49), channel_id=1, source_target_pairs={{0,8},{8,16},{16,24},{1,9},{9,17},{17,25},{2,10},{10,18},{18,26},{... | collective-permute-start | bytes 24584 | tf_op jit(solution)/shard_map/ppermute | solution.py:16
  39.4 3.5 %collective-permute-done.4 = f32[1,16,128]{2,1,0:T(8,128)S(1)} collective-permute-done((f32[1,16,128]{2,1,0:T(8,128)S(1)}, f32[1,16,128]{2,1,0:T(8,128)S(1)}, u32[]{:S(2)}, u32[]{:S(2)}) %collective-permute-start.4) | collective-permute-done | bytes 8224 | tf_op jit(solution)/shard_map/ppermute | solution.py:19
  43.0 4.5 %collective-permute-start.5 = (f32[10,1,128]{2,1,0:T(1,128)S(1)}, f32[10,1,128]{2,1,0:T(1,128)S(1)}, u32[]{:S(2)}, u32[]{:S(2)}) collective-permute-start(f32[10,1,128]{2,1,0:T(1,128)S(1)} %get-tuple-element.42), channel_id=1, source_target_pairs={{0,2},{2,4},{4,6},{1,3},{3,5},{5,7},{8,10},{10,12},{12,14},{9,11},... | collective-permute-start | bytes 15368 | tf_op jit(solution)/shard_map/ppermute | solution.py:16
  49.5 4.3 %collective-permute-done.6 = f32[10,1,128]{2,1,0:T(1,128)S(1)} collective-permute-done((f32[10,1,128]{2,1,0:T(1,128)S(1)}, f32[10,1,128]{2,1,0:T(1,128)S(1)}, u32[]{:S(2)}, u32[]{:S(2)}) %collective-permute-start.6) | collective-permute-done | bytes 5152 | tf_op jit(solution)/shard_map/ppermute | solution.py:19
  60.0 4.5 %collective-permute-start.9 = (f32[1,16,128]{2,1,0:T(8,128)S(1)}, f32[1,16,128]{2,1,0:T(8,128)S(1)}, u32[]{:S(2)}, u32[]{:S(2)}) collective-permute-start(f32[1,16,128]{2,1,0:T(8,128)S(1)} %get-tuple-element.47), channel_id=1, source_target_pairs={{0,8},{8,16},{16,24},{1,9},{9,17},{17,25},{2,10},{10,18},{18,26},{... | collective-permute-start | bytes 24584 | tf_op jit(solution)/shard_map/ppermute | solution.py:16
  65.9 4.8 %collective-permute-start.11 = (f32[10,1,128]{2,1,0:T(1,128)S(1)}, f32[10,1,128]{2,1,0:T(1,128)S(1)}, u32[]{:S(2)}, u32[]{:S(2)}) collective-permute-start(f32[10,1,128]{2,1,0:T(1,128)S(1)} %get-tuple-element.40), channel_id=1, source_target_pairs={{0,2},{2,4},{4,6},{1,3},{3,5},{5,7},{8,10},{10,12},{12,14},{9,11},... | collective-permute-start | bytes 15368 | tf_op jit(solution)/shard_map/ppermute | solution.py:16
  72.0 4.2 %collective-permute-done.12 = f32[10,1,128]{2,1,0:T(1,128)S(1)} collective-permute-done((f32[10,1,128]{2,1,0:T(1,128)S(1)}, f32[10,1,128]{2,1,0:T(1,128)S(1)}, u32[]{:S(2)}, u32[]{:S(2)}) %collective-permute-start.12) | collective-permute-done | bytes 5152 | tf_op jit(solution)/shard_map/ppermute | solution.py:19
  79.3 5.5 %reshape.693 = f32[4,2,8,2,64,2]{5,4,3,2,1,0:T(8,128)} reshape(f32[8,16,128]{2,1,0:T(8,128)S(1)} %get-tuple-element.23) | data formatting | bytes 131072 | tf_op jit(solution)/shard_map/reshape | solution.py:48
  84.8 5.5 %reshape.691 = f32[4,2,8,2,64,2]{5,4,3,2,1,0:T(8,128)} reshape(f32[8,16,128]{2,1,0:T(8,128)S(1)} %get-tuple-element.22) | data formatting | bytes 131072 | tf_op jit(solution)/shard_map/reshape | solution.py:48
  90.3 2.8 reduce_sum.350
  93.8 2.8 reduce_sum.348
  96.7 5.5 %reshape.689 = f32[4,2,8,2,64,2]{5,4,3,2,1,0:T(8,128)} reshape(f32[8,16,128]{2,1,0:T(8,128)S(1)} %get-tuple-element.46) | data formatting | bytes 131072 | tf_op jit(solution)/shard_map/reshape | solution.py:48
  102.2 2.8 reduce_sum.346
  105.2 5.5 %reshape.687 = f32[4,2,8,2,64,2]{5,4,3,2,1,0:T(8,128)} reshape(f32[8,16,128]{2,1,0:T(8,128)S(1)} %fusion.18) | data formatting | bytes 131072 | tf_op jit(solution)/shard_map/reshape | solution.py:48
  113.3 4.2 %collective-permute-start.15 = (f32[1,8,64]{2,1,0:T(8,128)S(1)}, f32[1,8,64]{2,1,0:T(8,128)S(1)}, u32[]{:S(2)}, u32[]{:S(2)}) collective-permute-start(f32[1,8,64]{2,1,0:T(8,128)S(1)} %get-tuple-element.73), channel_id=1, source_target_pairs={{0,8},{8,16},{16,24},{1,9},{9,17},{17,25},{2,10},{10,18},{18,26},{... | collective-permute-start | bytes 6152 | tf_op jit(solution)/shard_map/ppermute | solution.py:16
  119.0 4.0 %collective-permute-done.16 = f32[1,8,64]{2,1,0:T(8,128)S(1)} collective-permute-done((f32[1,8,64]{2,1,0:T(8,128)S(1)}, f32[1,8,64]{2,1,0:T(8,128)S(1)}, u32[]{:S(2)}, u32[]{:S(2)}) %collective-permute-start.16) | collective-permute-done | bytes 2080 | tf_op jit(solution)/shard_map/ppermute | solution.py:19
  123.0 2.8 collective-permute-start.17
  127.1 4.2 %collective-permute-done.18 = f32[6,1,64]{2,1,0:T(1,128)S(1)} collective-permute-done((f32[6,1,64]{2,1,0:T(1,128)S(1)}, f32[6,1,64]{2,1,0:T(1,128)S(1)}, u32[]{:S(2)}, u32[]{:S(2)}) %collective-permute-start.18) | collective-permute-done | bytes 1568 | tf_op jit(solution)/shard_map/ppermute | solution.py:19
  135.9 3.5 %collective-permute-start.21 = (f32[1,8,64]{2,1,0:T(8,128)S(1)}, f32[1,8,64]{2,1,0:T(8,128)S(1)}, u32[]{:S(2)}, u32[]{:S(2)}) collective-permute-start(f32[1,8,64]{2,1,0:T(8,128)S(1)} %get-tuple-element.71), channel_id=1, source_target_pairs={{0,8},{8,16},{16,24},{1,9},{9,17},{17,25},{2,10},{10,18},{18,26},{... | collective-permute-start | bytes 6152 | tf_op jit(solution)/shard_map/ppermute | solution.py:16
  141.4 3.5 %collective-permute-done.22 = f32[1,8,64]{2,1,0:T(8,128)S(1)} collective-permute-done((f32[1,8,64]{2,1,0:T(8,128)S(1)}, f32[1,8,64]{2,1,0:T(8,128)S(1)}, u32[]{:S(2)}, u32[]{:S(2)}) %collective-permute-start.22) | collective-permute-done | bytes 2080 | tf_op jit(solution)/shard_map/ppermute | solution.py:19
  144.9 2.8 collective-permute-start.23
  149.9 3.4 %collective-permute-done.24 = f32[6,1,64]{2,1,0:T(1,128)S(1)} collective-permute-done((f32[6,1,64]{2,1,0:T(1,128)S(1)}, f32[6,1,64]{2,1,0:T(1,128)S(1)}, u32[]{:S(2)}, u32[]{:S(2)}) %collective-permute-start.24) | collective-permute-done | bytes 1568 | tf_op jit(solution)/shard_map/ppermute | solution.py:19
  158.5 3.5 %collective-permute-start.27 = (f32[1,4,32]{2,1,0:T(4,128)S(1)}, f32[1,4,32]{2,1,0:T(4,128)S(1)}, u32[]{:S(2)}, u32[]{:S(2)}) collective-permute-start(f32[1,4,32]{2,1,0:T(4,128)S(1)} %get-tuple-element.85), channel_id=1, source_target_pairs={{0,8},{8,16},{16,24},{1,9},{9,17},{17,25},{2,10},{10,18},{18,26},{... | collective-permute-start | bytes 1544 | tf_op jit(solution)/shard_map/ppermute | solution.py:16
  163.5 4.0 %collective-permute-done.28 = f32[1,4,32]{2,1,0:T(4,128)S(1)} collective-permute-done((f32[1,4,32]{2,1,0:T(4,128)S(1)}, f32[1,4,32]{2,1,0:T(4,128)S(1)}, u32[]{:S(2)}, u32[]{:S(2)}) %collective-permute-start.28) | collective-permute-done | bytes 544 | tf_op jit(solution)/shard_map/ppermute | solution.py:19
  167.5 2.8 collective-permute-start.29
  171.7 4.2 %collective-permute-done.30 = f32[4,1,32]{2,1,0:T(1,128)S(1)} collective-permute-done((f32[4,1,32]{2,1,0:T(1,128)S(1)}, f32[4,1,32]{2,1,0:T(1,128)S(1)}, u32[]{:S(2)}, u32[]{:S(2)}) %collective-permute-start.30) | collective-permute-done | bytes 544 | tf_op jit(solution)/shard_map/ppermute | solution.py:19
  183.8 4.0 %collective-permute-done.34 = f32[1,4,32]{2,1,0:T(4,128)S(1)} collective-permute-done((f32[1,4,32]{2,1,0:T(4,128)S(1)}, f32[1,4,32]{2,1,0:T(4,128)S(1)}, u32[]{:S(2)}, u32[]{:S(2)}) %collective-permute-start.34) | collective-permute-done | bytes 544 | tf_op jit(solution)/shard_map/ppermute | solution.py:19
  187.8 2.8 collective-permute-start.35
  192.1 4.0 %collective-permute-done.36 = f32[4,1,32]{2,1,0:T(1,128)S(1)} collective-permute-done((f32[4,1,32]{2,1,0:T(1,128)S(1)}, f32[4,1,32]{2,1,0:T(1,128)S(1)}, u32[]{:S(2)}, u32[]{:S(2)}) %collective-permute-start.36) | collective-permute-done | bytes 544 | tf_op jit(solution)/shard_map/ppermute | solution.py:19
  203.2 2.8 collective-permute-done.40
  206.1 3.8 %collective-permute-done.41 = f32[4,7,1,2,16]{4,3,1,2,0:T(2,128)S(1)} collective-permute-done((f32[4,7,1,2,16]{4,3,1,2,0:T(2,128)S(1)}, f32[4,7,1,2,16]{4,3,1,2,0:T(2,128)S(1)}, u32[]{:S(2)}, u32[]{:S(2)}) %collective-permute-start.41) | collective-permute-done | bytes 3616 | tf_op jit(solution)/shard_map/ppermute | solution.py:112
  210.1 4.1 %collective-permute-done.42 = f32[8,7,1,2,16]{4,3,1,2,0:T(2,128)S(1)} collective-permute-done((f32[8,7,1,2,16]{4,3,1,2,0:T(2,128)S(1)}, f32[8,7,1,2,16]{4,3,1,2,0:T(2,128)S(1)}, u32[]{:S(2)}, u32[]{:S(2)}) %collective-permute-start.42) | collective-permute-done | bytes 7200 | tf_op jit(solution)/shard_map/ppermute | solution.py:112
  214.4 6.6 %collective-permute-done.43 = f32[16,7,1,2,16]{4,3,1,2,0:T(2,128)S(1)} collective-permute-done((f32[16,7,1,2,16]{4,3,1,2,0:T(2,128)S(1)}, f32[16,7,1,2,16]{4,3,1,2,0:T(2,128)S(1)}, u32[]{:S(2)}, u32[]{:S(2)}) %collective-permute-start.43) | collective-permute-done | bytes 14368 | tf_op jit(solution)/shard_map/ppermute | solution.py:112
  248.5 4.2 %collective-permute-done.45 = f32[1,4,32]{2,1,0:T(4,128)S(1)} collective-permute-done((f32[1,4,32]{2,1,0:T(4,128)S(1)}, f32[1,4,32]{2,1,0:T(4,128)S(1)}, u32[]{:S(2)}, u32[]{:S(2)}) %collective-permute-start.45) | collective-permute-done | bytes 544 | tf_op jit(solution)/shard_map/ppermute | solution.py:19
  252.7 2.8 collective-permute-start.46
  256.8 4.2 %collective-permute-done.47 = f32[4,1,32]{2,1,0:T(1,128)S(1)} collective-permute-done((f32[4,1,32]{2,1,0:T(1,128)S(1)}, f32[4,1,32]{2,1,0:T(1,128)S(1)}, u32[]{:S(2)}, u32[]{:S(2)}) %collective-permute-start.47) | collective-permute-done | bytes 544 | tf_op jit(solution)/shard_map/ppermute | solution.py:19
  269.8 4.2 %collective-permute-done.51 = f32[1,8,64]{2,1,0:T(8,128)S(1)} collective-permute-done((f32[1,8,64]{2,1,0:T(8,128)S(1)}, f32[1,8,64]{2,1,0:T(8,128)S(1)}, u32[]{:S(2)}, u32[]{:S(2)}) %collective-permute-start.51) | collective-permute-done | bytes 2080 | tf_op jit(solution)/shard_map/ppermute | solution.py:19
  274.0 3.1 collective-permute-start.52
  278.4 4.2 %collective-permute-done.53 = f32[6,1,64]{2,1,0:T(1,128)S(1)} collective-permute-done((f32[6,1,64]{2,1,0:T(1,128)S(1)}, f32[6,1,64]{2,1,0:T(1,128)S(1)}, u32[]{:S(2)}, u32[]{:S(2)}) %collective-permute-start.53) | collective-permute-done | bytes 1568 | tf_op jit(solution)/shard_map/ppermute | solution.py:19
  289.8 4.0 %reshape.696 = f32[8,16,128]{2,1,0:T(8,128)S(1)} reshape(f32[4,2,8,2,64,2]{5,4,3,2,1,0:T(8,128)} %broadcast_in_dim.33) | data formatting | bytes 131072 | tf_op jit(solution)/shard_map/reshape | solution.py:75
  297.1 4.2 %collective-permute-done.57 = f32[1,16,128]{2,1,0:T(8,128)S(1)} collective-permute-done((f32[1,16,128]{2,1,0:T(8,128)S(1)}, f32[1,16,128]{2,1,0:T(8,128)S(1)}, u32[]{:S(2)}, u32[]{:S(2)}) %collective-permute-start.57) | collective-permute-done | bytes 8224 | tf_op jit(solution)/shard_map/ppermute | solution.py:19
  301.3 2.8 collective-permute-start.58
  305.4 4.2 %collective-permute-done.59 = f32[10,1,128]{2,1,0:T(1,128)S(1)} collective-permute-done((f32[10,1,128]{2,1,0:T(1,128)S(1)}, f32[10,1,128]{2,1,0:T(1,128)S(1)}, u32[]{:S(2)}, u32[]{:S(2)}) %collective-permute-start.59) | collective-permute-done | bytes 5152 | tf_op jit(solution)/shard_map/ppermute | solution.py:19
  (266 shorter events, 104.9 us)
Async XLA Ops:
  0.7 30.9 %collective-permute-start = (f32[1,16,128]{2,1,0:T(8,128)S(1)}, f32[1,16,128]{2,1,0:T(8,128)S(1)}, u32[]{:S(2)}, u32[]{:S(2)}) collective-permute-start(f32[1,16,128]{2,1,0:T(8,128)S(1)} %slice.587), channel_id=1, source_target_pairs={{8,0},{16,8},{24,16},{9,1},{17,9},{25,17},{10,2},{18,10},{26,18},{... | collective-permute-start | bytes 24584 | tf_op jit(solution)/shard_map/ppermute | solution.py:27
  2.0 29.6 %collective-permute-start.2 = (f32[8,16,1]{2,1,0:T(8,128)}, f32[8,16,1]{2,1,0:T(8,128)S(1)}, u32[]{:S(2)}, u32[]{:S(2)}) collective-permute-start(f32[8,16,1]{2,1,0:T(8,128)} %bitcast.313), channel_id=1, source_target_pairs={{1,0},{3,2},{5,4},{7,6},{9,8},{11,10},{13,12},{15,14},{17,16},{19,... | collective-permute-start | bytes 1544 | tf_op jit(solution)/shard_map/ppermute | solution.py:27
  4.1 27.6 %collective-permute-start.1 = (f32[8,1,128]{2,1,0:T(1,128)S(1)}, f32[8,1,128]{2,1,0:T(1,128)S(1)}, u32[]{:S(2)}, u32[]{:S(2)}) collective-permute-start(f32[8,1,128]{2,1,0:T(1,128)S(1)} %slice.589), channel_id=1, source_target_pairs={{2,0},{4,2},{6,4},{3,1},{5,3},{7,5},{10,8},{12,10},{14,12},{11,9},... | collective-permute-start | bytes 12296 | tf_op jit(solution)/shard_map/ppermute | solution.py:27
  31.8 7.6 %collective-permute-start.3 = (f32[1,16,128]{2,1,0:T(8,128)S(1)}, f32[1,16,128]{2,1,0:T(8,128)S(1)}, u32[]{:S(2)}, u32[]{:S(2)}) collective-permute-start(f32[1,16,128]{2,1,0:T(8,128)S(1)} %get-tuple-element.49), channel_id=1, source_target_pairs={{0,8},{8,16},{16,24},{1,9},{9,17},{17,25},{2,10},{10,18},{18,26},{... | collective-permute-start | bytes 24584 | tf_op jit(solution)/shard_map/ppermute | solution.py:16
  37.4 5.5 %collective-permute-start.4 = (f32[1,16,128]{2,1,0:T(8,128)S(1)}, f32[1,16,128]{2,1,0:T(8,128)S(1)}, u32[]{:S(2)}, u32[]{:S(2)}) collective-permute-start(f32[1,16,128]{2,1,0:T(8,128)S(1)} %get-tuple-element.50), channel_id=1, source_target_pairs={{8,0},{16,8},{24,16},{9,1},{17,9},{25,17},{10,2},{18,10},{26,18},{... | collective-permute-start | bytes 24584 | tf_op jit(solution)/shard_map/ppermute | solution.py:19
  43.0 6.6 %collective-permute-start.5 = (f32[10,1,128]{2,1,0:T(1,128)S(1)}, f32[10,1,128]{2,1,0:T(1,128)S(1)}, u32[]{:S(2)}, u32[]{:S(2)}) collective-permute-start(f32[10,1,128]{2,1,0:T(1,128)S(1)} %get-tuple-element.42), channel_id=1, source_target_pairs={{0,2},{2,4},{4,6},{1,3},{3,5},{5,7},{8,10},{10,12},{12,14},{9,11},... | collective-permute-start | bytes 15368 | tf_op jit(solution)/shard_map/ppermute | solution.py:16
  47.5 6.3 %collective-permute-start.6 = (f32[10,1,128]{2,1,0:T(1,128)S(1)}, f32[10,1,128]{2,1,0:T(1,128)S(1)}, u32[]{:S(2)}, u32[]{:S(2)}) collective-permute-start(f32[10,1,128]{2,1,0:T(1,128)S(1)} %get-tuple-element.43), channel_id=1, source_target_pairs={{2,0},{4,2},{6,4},{3,1},{5,3},{7,5},{10,8},{12,10},{14,12},{11,9},... | collective-permute-start | bytes 15368 | tf_op jit(solution)/shard_map/ppermute | solution.py:19
  55.3 3.2 %collective-permute-start.8 = (f32[10,18,1]{2,1,0:T(8,128)S(1)}, f32[10,18,1]{2,1,0:T(8,128)S(1)}, u32[]{:S(2)}, u32[]{:S(2)}) collective-permute-start(f32[10,18,1]{2,1,0:T(8,128)S(1)} %get-tuple-element.37), channel_id=1, source_target_pairs={{1,0},{3,2},{5,4},{7,6},{9,8},{11,10},{13,12},{15,14},{17,16},{19,... | collective-permute-start | bytes 2168 | tf_op jit(solution)/shard_map/ppermute | solution.py:19
  58.7 6.6 %collective-permute-start.10 = (f32[1,16,128]{2,1,0:T(8,128)S(1)}, f32[1,16,128]{2,1,0:T(8,128)S(1)}, u32[]{:S(2)}, u32[]{:S(2)}) collective-permute-start(f32[1,16,128]{2,1,0:T(8,128)S(1)} %get-tuple-element.48), channel_id=1, source_target_pairs={{8,0},{16,8},{24,16},{9,1},{17,9},{25,17},{10,2},{18,10},{26,18},{... | collective-permute-start | bytes 24584 | tf_op jit(solution)/shard_map/ppermute | solution.py:19
  60.0 5.9 %collective-permute-start.9 = (f32[1,16,128]{2,1,0:T(8,128)S(1)}, f32[1,16,128]{2,1,0:T(8,128)S(1)}, u32[]{:S(2)}, u32[]{:S(2)}) collective-permute-start(f32[1,16,128]{2,1,0:T(8,128)S(1)} %get-tuple-element.47), channel_id=1, source_target_pairs={{0,8},{8,16},{16,24},{1,9},{9,17},{17,25},{2,10},{10,18},{18,26},{... | collective-permute-start | bytes 24584 | tf_op jit(solution)/shard_map/ppermute | solution.py:16
  65.9 6.1 %collective-permute-start.11 = (f32[10,1,128]{2,1,0:T(1,128)S(1)}, f32[10,1,128]{2,1,0:T(1,128)S(1)}, u32[]{:S(2)}, u32[]{:S(2)}) collective-permute-start(f32[10,1,128]{2,1,0:T(1,128)S(1)} %get-tuple-element.40), channel_id=1, source_target_pairs={{0,2},{2,4},{4,6},{1,3},{3,5},{5,7},{8,10},{10,12},{12,14},{9,11},... | collective-permute-start | bytes 15368 | tf_op jit(solution)/shard_map/ppermute | solution.py:16
  70.7 5.5 %collective-permute-start.12 = (f32[10,1,128]{2,1,0:T(1,128)S(1)}, f32[10,1,128]{2,1,0:T(1,128)S(1)}, u32[]{:S(2)}, u32[]{:S(2)}) collective-permute-start(f32[10,1,128]{2,1,0:T(1,128)S(1)} %get-tuple-element.41), channel_id=1, source_target_pairs={{2,0},{4,2},{6,4},{3,1},{5,3},{7,5},{10,8},{12,10},{14,12},{11,9},... | collective-permute-start | bytes 15368 | tf_op jit(solution)/shard_map/ppermute | solution.py:19
  76.3 28.7 %collective-permute-start.13 = (f32[10,18,1]{2,1,0:T(8,128)S(1)}, f32[10,18,1]{2,1,0:T(8,128)S(1)}, u32[]{:S(2)}, u32[]{:S(2)}) collective-permute-start(f32[10,18,1]{2,1,0:T(8,128)S(1)} %get-tuple-element.34), channel_id=1, source_target_pairs={{0,1},{2,3},{4,5},{6,7},{8,9},{10,11},{12,13},{14,15},{16,17},{18,... | collective-permute-start | bytes 2168 | tf_op jit(solution)/shard_map/ppermute | solution.py:16
  77.6 27.4 %collective-permute-start.14 = (f32[10,18,1]{2,1,0:T(8,128)S(1)}, f32[10,18,1]{2,1,0:T(8,128)S(1)}, u32[]{:S(2)}, u32[]{:S(2)}) collective-permute-start(f32[10,18,1]{2,1,0:T(8,128)S(1)} %get-tuple-element.35), channel_id=1, source_target_pairs={{1,0},{3,2},{5,4},{7,6},{9,8},{11,10},{13,12},{15,14},{17,16},{19,... | collective-permute-start | bytes 2168 | tf_op jit(solution)/shard_map/ppermute | solution.py:19
  113.3 5.7 %collective-permute-start.15 = (f32[1,8,64]{2,1,0:T(8,128)S(1)}, f32[1,8,64]{2,1,0:T(8,128)S(1)}, u32[]{:S(2)}, u32[]{:S(2)}) collective-permute-start(f32[1,8,64]{2,1,0:T(8,128)S(1)} %get-tuple-element.73), channel_id=1, source_target_pairs={{0,8},{8,16},{16,24},{1,9},{9,17},{17,25},{2,10},{10,18},{18,26},{... | collective-permute-start | bytes 6152 | tf_op jit(solution)/shard_map/ppermute | solution.py:16
  117.5 5.5 %collective-permute-start.16 = (f32[1,8,64]{2,1,0:T(8,128)S(1)}, f32[1,8,64]{2,1,0:T(8,128)S(1)}, u32[]{:S(2)}, u32[]{:S(2)}) collective-permute-start(f32[1,8,64]{2,1,0:T(8,128)S(1)} %get-tuple-element.74), channel_id=1, source_target_pairs={{8,0},{16,8},{24,16},{9,1},{17,9},{25,17},{10,2},{18,10},{26,18},{... | collective-permute-start | bytes 6152 | tf_op jit(solution)/shard_map/ppermute | solution.py:19
  123.0 4.1 %collective-permute-start.17 = (f32[6,1,64]{2,1,0:T(1,128)S(1)}, f32[6,1,64]{2,1,0:T(1,128)S(1)}, u32[]{:S(2)}, u32[]{:S(2)}) collective-permute-start(f32[6,1,64]{2,1,0:T(1,128)S(1)} %get-tuple-element.61), channel_id=1, source_target_pairs={{0,2},{2,4},{4,6},{1,3},{3,5},{5,7},{8,10},{10,12},{12,14},{9,11},... | collective-permute-start | bytes 4616 | tf_op jit(solution)/shard_map/ppermute | solution.py:16
  125.8 5.5 %collective-permute-start.18 = (f32[6,1,64]{2,1,0:T(1,128)S(1)}, f32[6,1,64]{2,1,0:T(1,128)S(1)}, u32[]{:S(2)}, u32[]{:S(2)}) collective-permute-start(f32[6,1,64]{2,1,0:T(1,128)S(1)} %get-tuple-element.62), channel_id=1, source_target_pairs={{2,0},{4,2},{6,4},{3,1},{5,3},{7,5},{10,8},{12,10},{14,12},{11,9},... | collective-permute-start | bytes 4616 | tf_op jit(solution)/shard_map/ppermute | solution.py:19
  132.7 3.1 collective-permute-start.20
  135.9 5.5 %collective-permute-start.21 = (f32[1,8,64]{2,1,0:T(8,128)S(1)}, f32[1,8,64]{2,1,0:T(8,128)S(1)}, u32[]{:S(2)}, u32[]{:S(2)}) collective-permute-start(f32[1,8,64]{2,1,0:T(8,128)S(1)} %get-tuple-element.71), channel_id=1, source_target_pairs={{0,8},{8,16},{16,24},{1,9},{9,17},{17,25},{2,10},{10,18},{18,26},{... | collective-permute-start | bytes 6152 | tf_op jit(solution)/shard_map/ppermute | solution.py:16
  139.4 5.5 %collective-permute-start.22 = (f32[1,8,64]{2,1,0:T(8,128)S(1)}, f32[1,8,64]{2,1,0:T(8,128)S(1)}, u32[]{:S(2)}, u32[]{:S(2)}) collective-permute-start(f32[1,8,64]{2,1,0:T(8,128)S(1)} %get-tuple-element.72), channel_id=1, source_target_pairs={{8,0},{16,8},{24,16},{9,1},{17,9},{25,17},{10,2},{18,10},{26,18},{... | collective-permute-start | bytes 6152 | tf_op jit(solution)/shard_map/ppermute | solution.py:19
  144.9 4.9 %collective-permute-start.23 = (f32[6,1,64]{2,1,0:T(1,128)S(1)}, f32[6,1,64]{2,1,0:T(1,128)S(1)}, u32[]{:S(2)}, u32[]{:S(2)}) collective-permute-start(f32[6,1,64]{2,1,0:T(1,128)S(1)} %get-tuple-element.59), channel_id=1, source_target_pairs={{0,2},{2,4},{4,6},{1,3},{3,5},{5,7},{8,10},{10,12},{12,14},{9,11},... | collective-permute-start | bytes 4616 | tf_op jit(solution)/shard_map/ppermute | solution.py:16
  147.7 5.5 %collective-permute-start.24 = (f32[6,1,64]{2,1,0:T(1,128)S(1)}, f32[6,1,64]{2,1,0:T(1,128)S(1)}, u32[]{:S(2)}, u32[]{:S(2)}) collective-permute-start(f32[6,1,64]{2,1,0:T(1,128)S(1)} %get-tuple-element.60), channel_id=1, source_target_pairs={{2,0},{4,2},{6,4},{3,1},{5,3},{7,5},{10,8},{12,10},{14,12},{11,9},... | collective-permute-start | bytes 4616 | tf_op jit(solution)/shard_map/ppermute | solution.py:19
  153.3 3.3 %collective-permute-start.25 = (f32[6,10,1]{2,1,0:T(8,128)S(1)}, f32[6,10,1]{2,1,0:T(8,128)S(1)}, u32[]{:S(2)}, u32[]{:S(2)}) collective-permute-start(f32[6,10,1]{2,1,0:T(8,128)S(1)} %get-tuple-element.53), channel_id=1, source_target_pairs={{0,1},{2,3},{4,5},{6,7},{8,9},{10,11},{12,13},{14,15},{16,17},{18,... | collective-permute-start | bytes 728 | tf_op jit(solution)/shard_map/ppermute | solution.py:16
  158.5 5.0 %collective-permute-start.27 = (f32[1,4,32]{2,1,0:T(4,128)S(1)}, f32[1,4,32]{2,1,0:T(4,128)S(1)}, u32[]{:S(2)}, u32[]{:S(2)}) collective-permute-start(f32[1,4,32]{2,1,0:T(4,128)S(1)} %get-tuple-element.85), channel_id=1, source_target_pairs={{0,8},{8,16},{16,24},{1,9},{9,17},{17,25},{2,10},{10,18},{18,26},{... | collective-permute-start | bytes 1544 | tf_op jit(solution)/shard_map/ppermute | solution.py:16
  162.0 5.5 %collective-permute-start.28 = (f32[1,4,32]{2,1,0:T(4,128)S(1)}, f32[1,4,32]{2,1,0:T(4,128)S(1)}, u32[]{:S(2)}, u32[]{:S(2)}) collective-permute-start(f32[1,4,32]{2,1,0:T(4,128)S(1)} %get-tuple-element.86), channel_id=1, source_target_pairs={{8,0},{16,8},{24,16},{9,1},{17,9},{25,17},{10,2},{18,10},{26,18},{... | collective-permute-start | bytes 1544 | tf_op jit(solution)/shard_map/ppermute | solution.py:19
  167.5 4.1 %collective-permute-start.29 = (f32[4,1,32]{2,1,0:T(1,128)S(1)}, f32[4,1,32]{2,1,0:T(1,128)S(1)}, u32[]{:S(2)}, u32[]{:S(2)}) collective-permute-start(f32[4,1,32]{2,1,0:T(1,128)S(1)} %get-tuple-element.79), channel_id=1, source_target_pairs={{0,2},{2,4},{4,6},{1,3},{3,5},{5,7},{8,10},{10,12},{12,14},{9,11},... | collective-permute-start | bytes 1544 | tf_op jit(solution)/shard_map/ppermute | solution.py:16
  170.3 5.5 %collective-permute-start.30 = (f32[4,1,32]{2,1,0:T(1,128)S(1)}, f32[4,1,32]{2,1,0:T(1,128)S(1)}, u32[]{:S(2)}, u32[]{:S(2)}) collective-permute-start(f32[4,1,32]{2,1,0:T(1,128)S(1)} %get-tuple-element.80), channel_id=1, source_target_pairs={{2,0},{4,2},{6,4},{3,1},{5,3},{7,5},{10,8},{12,10},{14,12},{11,9},... | collective-permute-start | bytes 1544 | tf_op jit(solution)/shard_map/ppermute | solution.py:19
  180.4 3.4 %collective-permute-start.33 = (f32[1,4,32]{2,1,0:T(4,128)S(1)}, f32[1,4,32]{2,1,0:T(4,128)S(1)}, u32[]{:S(2)}, u32[]{:S(2)}) collective-permute-start(f32[1,4,32]{2,1,0:T(4,128)S(1)} %get-tuple-element.83), channel_id=1, source_target_pairs={{0,8},{8,16},{16,24},{1,9},{9,17},{17,25},{2,10},{10,18},{18,26},{... | collective-permute-start | bytes 1544 | tf_op jit(solution)/shard_map/ppermute | solution.py:16
  182.3 5.5 %collective-permute-start.34 = (f32[1,4,32]{2,1,0:T(4,128)S(1)}, f32[1,4,32]{2,1,0:T(4,128)S(1)}, u32[]{:S(2)}, u32[]{:S(2)}) collective-permute-start(f32[1,4,32]{2,1,0:T(4,128)S(1)} %get-tuple-element.84), channel_id=1, source_target_pairs={{8,0},{16,8},{24,16},{9,1},{17,9},{25,17},{10,2},{18,10},{26,18},{... | collective-permute-start | bytes 1544 | tf_op jit(solution)/shard_map/ppermute | solution.py:19
  187.8 4.3 %collective-permute-start.35 = (f32[4,1,32]{2,1,0:T(1,128)S(1)}, f32[4,1,32]{2,1,0:T(1,128)S(1)}, u32[]{:S(2)}, u32[]{:S(2)}) collective-permute-start(f32[4,1,32]{2,1,0:T(1,128)S(1)} %get-tuple-element.77), channel_id=1, source_target_pairs={{0,2},{2,4},{4,6},{1,3},{3,5},{5,7},{8,10},{10,12},{12,14},{9,11},... | collective-permute-start | bytes 1544 | tf_op jit(solution)/shard_map/ppermute | solution.py:16
  190.6 5.5 %collective-permute-start.36 = (f32[4,1,32]{2,1,0:T(1,128)S(1)}, f32[4,1,32]{2,1,0:T(1,128)S(1)}, u32[]{:S(2)}, u32[]{:S(2)}) collective-permute-start(f32[4,1,32]{2,1,0:T(1,128)S(1)} %get-tuple-element.78), channel_id=1, source_target_pairs={{2,0},{4,2},{6,4},{3,1},{5,3},{7,5},{10,8},{12,10},{14,12},{11,9},... | collective-permute-start | bytes 1544 | tf_op jit(solution)/shard_map/ppermute | solution.py:19
  202.2 3.8 %collective-permute-start.40 = (f32[2,7,1,2,16]{4,3,1,2,0:T(2,128)S(1)}, f32[2,7,1,2,16]{4,3,1,2,0:T(2,128)S(1)}, u32[]{:S(2)}, u32[]{:S(2)}) collective-permute-start(f32[2,7,1,2,16]{4,3,1,2,0:T(2,128)S(1)} %maximum_select_fusion.5), channel_id=1, source_target_pairs={{0,2},{1,3},{2,0},{3,1},{4,6},{5,7},{6,4},{7,5},{8,10},{9,11},{10,... | collective-permute-start | bytes 5384 | tf_op jit(solution)/shard_map/ppermute | solution.py:112
  206.0 3.9 %collective-permute-start.41 = (f32[4,7,1,2,16]{4,3,1,2,0:T(2,128)S(1)}, f32[4,7,1,2,16]{4,3,1,2,0:T(2,128)S(1)}, u32[]{:S(2)}, u32[]{:S(2)}) collective-permute-start(f32[4,7,1,2,16]{4,3,1,2,0:T(2,128)S(1)} %fusion.48), channel_id=1, source_target_pairs={{0,4},{1,5},{2,6},{3,7},{4,0},{5,1},{6,2},{7,3},{8,12},{9,13},{10,... | collective-permute-start | bytes 10760 | tf_op jit(solution)/shard_map/ppermute | solution.py:112
  210.0 4.2 %collective-permute-start.42 = (f32[8,7,1,2,16]{4,3,1,2,0:T(2,128)S(1)}, f32[8,7,1,2,16]{4,3,1,2,0:T(2,128)S(1)}, u32[]{:S(2)}, u32[]{:S(2)}) collective-permute-start(f32[8,7,1,2,16]{4,3,1,2,0:T(2,128)S(1)} %fusion.47), channel_id=1, source_target_pairs={{0,8},{1,9},{2,10},{3,11},{4,12},{5,13},{6,14},{7,15},{8,0},{9,1},... | collective-permute-start | bytes 21512 | tf_op jit(solution)/shard_map/ppermute | solution.py:112
  214.3 6.7 %collective-permute-start.43 = (f32[16,7,1,2,16]{4,3,1,2,0:T(2,128)S(1)}, f32[16,7,1,2,16]{4,3,1,2,0:T(2,128)S(1)}, u32[]{:S(2)}, u32[]{:S(2)}) collective-permute-start(f32[16,7,1,2,16]{4,3,1,2,0:T(2,128)S(1)} %maximum_select_fusion.1), channel_id=1, source_target_pairs={{0,16},{1,17},{2,18},{3,19},{4,20},{5,21},{6,22},{7,23},{8,24},{9,... | collective-permute-start | bytes 43016 | tf_op jit(solution)/shard_map/ppermute | solution.py:112
  247.2 5.5 %collective-permute-start.45 = (f32[1,4,32]{2,1,0:T(4,128)S(1)}, f32[1,4,32]{2,1,0:T(4,128)S(1)}, u32[]{:S(2)}, u32[]{:S(2)}) collective-permute-start(f32[1,4,32]{2,1,0:T(4,128)S(1)} %get-tuple-element.82), channel_id=1, source_target_pairs={{8,0},{16,8},{24,16},{9,1},{17,9},{25,17},{10,2},{18,10},{26,18},{... | collective-permute-start | bytes 1544 | tf_op jit(solution)/shard_map/ppermute | solution.py:19
  252.7 4.1 %collective-permute-start.46 = (f32[4,1,32]{2,1,0:T(1,128)S(1)}, f32[4,1,32]{2,1,0:T(1,128)S(1)}, u32[]{:S(2)}, u32[]{:S(2)}) collective-permute-start(f32[4,1,32]{2,1,0:T(1,128)S(1)} %get-tuple-element.75), channel_id=1, source_target_pairs={{0,2},{2,4},{4,6},{1,3},{3,5},{5,7},{8,10},{10,12},{12,14},{9,11},... | collective-permute-start | bytes 1544 | tf_op jit(solution)/shard_map/ppermute | solution.py:16
  255.5 5.5 %collective-permute-start.47 = (f32[4,1,32]{2,1,0:T(1,128)S(1)}, f32[4,1,32]{2,1,0:T(1,128)S(1)}, u32[]{:S(2)}, u32[]{:S(2)}) collective-permute-start(f32[4,1,32]{2,1,0:T(1,128)S(1)} %get-tuple-element.76), channel_id=1, source_target_pairs={{2,0},{4,2},{6,4},{3,1},{5,3},{7,5},{10,8},{12,10},{14,12},{11,9},... | collective-permute-start | bytes 1544 | tf_op jit(solution)/shard_map/ppermute | solution.py:19
  265.9 3.9 %collective-permute-start.50 = (f32[1,8,64]{2,1,0:T(8,128)S(1)}, f32[1,8,64]{2,1,0:T(8,128)S(1)}, u32[]{:S(2)}, u32[]{:S(2)}) collective-permute-start(f32[1,8,64]{2,1,0:T(8,128)S(1)} %get-tuple-element.63), channel_id=1, source_target_pairs={{0,8},{8,16},{16,24},{1,9},{9,17},{17,25},{2,10},{10,18},{18,26},{... | collective-permute-start | bytes 6152 | tf_op jit(solution)/shard_map/ppermute | solution.py:16
  268.5 5.5 %collective-permute-start.51 = (f32[1,8,64]{2,1,0:T(8,128)S(1)}, f32[1,8,64]{2,1,0:T(8,128)S(1)}, u32[]{:S(2)}, u32[]{:S(2)}) collective-permute-start(f32[1,8,64]{2,1,0:T(8,128)S(1)} %get-tuple-element.64), channel_id=1, source_target_pairs={{8,0},{16,8},{24,16},{9,1},{17,9},{25,17},{10,2},{18,10},{26,18},{... | collective-permute-start | bytes 6152 | tf_op jit(solution)/shard_map/ppermute | solution.py:19
  274.0 4.4 %collective-permute-start.52 = (f32[6,1,64]{2,1,0:T(1,128)S(1)}, f32[6,1,64]{2,1,0:T(1,128)S(1)}, u32[]{:S(2)}, u32[]{:S(2)}) collective-permute-start(f32[6,1,64]{2,1,0:T(1,128)S(1)} %get-tuple-element.57), channel_id=1, source_target_pairs={{0,2},{2,4},{4,6},{1,3},{3,5},{5,7},{8,10},{10,12},{12,14},{9,11},... | collective-permute-start | bytes 4616 | tf_op jit(solution)/shard_map/ppermute | solution.py:16
  277.1 5.5 %collective-permute-start.53 = (f32[6,1,64]{2,1,0:T(1,128)S(1)}, f32[6,1,64]{2,1,0:T(1,128)S(1)}, u32[]{:S(2)}, u32[]{:S(2)}) collective-permute-start(f32[6,1,64]{2,1,0:T(1,128)S(1)} %get-tuple-element.58), channel_id=1, source_target_pairs={{2,0},{4,2},{6,4},{3,1},{5,3},{7,5},{10,8},{12,10},{14,12},{11,9},... | collective-permute-start | bytes 4616 | tf_op jit(solution)/shard_map/ppermute | solution.py:19
  293.8 3.3 %collective-permute-start.56 = (f32[1,16,128]{2,1,0:T(8,128)S(1)}, f32[1,16,128]{2,1,0:T(8,128)S(1)}, u32[]{:S(2)}, u32[]{:S(2)}) collective-permute-start(f32[1,16,128]{2,1,0:T(8,128)S(1)} %get-tuple-element.44), channel_id=1, source_target_pairs={{0,8},{8,16},{16,24},{1,9},{9,17},{17,25},{2,10},{10,18},{18,26},{... | collective-permute-start | bytes 24584 | tf_op jit(solution)/shard_map/ppermute | solution.py:16
  295.7 5.5 %collective-permute-start.57 = (f32[1,16,128]{2,1,0:T(8,128)S(1)}, f32[1,16,128]{2,1,0:T(8,128)S(1)}, u32[]{:S(2)}, u32[]{:S(2)}) collective-permute-start(f32[1,16,128]{2,1,0:T(8,128)S(1)} %get-tuple-element.45), channel_id=1, source_target_pairs={{8,0},{16,8},{24,16},{9,1},{17,9},{25,17},{10,2},{18,10},{26,18},{... | collective-permute-start | bytes 24584 | tf_op jit(solution)/shard_map/ppermute | solution.py:19
  301.3 4.2 %collective-permute-start.58 = (f32[10,1,128]{2,1,0:T(1,128)S(1)}, f32[10,1,128]{2,1,0:T(1,128)S(1)}, u32[]{:S(2)}, u32[]{:S(2)}) collective-permute-start(f32[10,1,128]{2,1,0:T(1,128)S(1)} %get-tuple-element.38), channel_id=1, source_target_pairs={{0,2},{2,4},{4,6},{1,3},{3,5},{5,7},{8,10},{10,12},{12,14},{9,11},... | collective-permute-start | bytes 15368 | tf_op jit(solution)/shard_map/ppermute | solution.py:16
  304.1 5.5 %collective-permute-start.59 = (f32[10,1,128]{2,1,0:T(1,128)S(1)}, f32[10,1,128]{2,1,0:T(1,128)S(1)}, u32[]{:S(2)}, u32[]{:S(2)}) collective-permute-start(f32[10,1,128]{2,1,0:T(1,128)S(1)} %get-tuple-element.39), channel_id=1, source_target_pairs={{2,0},{4,2},{6,4},{3,1},{5,3},{7,5},{10,8},{12,10},{14,12},{11,9},... | collective-permute-start | bytes 15368 | tf_op jit(solution)/shard_map/ppermute | solution.py:19
  311.1 3.2 %collective-permute-start.61 = (f32[10,18,1]{2,1,0:T(8,128)S(1)}, f32[10,18,1]{2,1,0:T(8,128)S(1)}, u32[]{:S(2)}, u32[]{:S(2)}) collective-permute-start(f32[10,18,1]{2,1,0:T(8,128)S(1)} %get-tuple-element.33), channel_id=1, source_target_pairs={{1,0},{3,2},{5,4},{7,6},{9,8},{11,10},{13,12},{15,14},{17,16},{19,... | collective-permute-start | bytes 2168 | tf_op jit(solution)/shard_map/ppermute | solution.py:19
  (18 other events, 70.1 us)
